TPU v7x, 32 devices: a whole 2x2x4 slice. The times are simulated.
32 devices in a mesh: slab: 16 (over z, x, core), tpl: 2 (over y).
Axes of the slice: x: 2, y: 2, z: 4, core: 2. Of those that a mesh axis runs over, the one named last changes fastest.
Arguments:
- data: bfloat16 [128, 3, 16384], P('tpl', None, 'slab')
- templates: bfloat16 [64, 8, 3, 512], P(('tpl', 'slab')), may hold values from -6 to 6
- stations: int32 [64, 8], P(('tpl', 'slab')), may hold values from 0 to 127
- shifts: int32 [64, 8], P(('tpl', 'slab')), may hold values from 0 to 255
- used: int32 [64], P(('tpl', 'slab')), may hold values from 1 to 8
Outputs:
- detection: float32 [64, 16384], P('tpl', 'slab')
Inputs may be any that keep to these rules, and one draw needn't show every extreme that they name: Only the first used[j] slots of template j count; stations may repeat.
All inputs are finite; a program needn't handle non-finite values.
Results may differ from a plain program's by a relative error of at most 0.0065.
Values may be sent and summed in bfloat16 or wider, within the bound.
A program may use at most 256 MiB of HBM per device.

v0:
```python
import math

import jax
import jax.numpy as jnp
from jax import lax
from jax.sharding import PartitionSpec as P

MAXSHIFT = 256


EPS = 1e-05


def passed_along(value, axis, steps):
    count = lax.axis_size(axis)
    initial, last = (max(0, -steps), min(count, count - steps))
    return lax.ppermute(value, axis, [(source, source + steps) for source in range(initial, last)])


def normalize(templates):
    span = templates.shape[-1]
    rows = templates.astype(jnp.float32)
    centered = rows - jnp.mean(rows, axis=-1, keepdims=True)
    rms = jnp.sqrt(jnp.mean(centered * centered, axis=-1, keepdims=True) + EPS)
    return (centered / (rms * math.sqrt(span))).astype(jnp.bfloat16)


def box_sums(values, span):
    width = values.shape[-1]
    block_len = span // 8
    nblocks = -(-width // block_len) + 8
    lead = values.shape[:-1]
    padded = jnp.pad(values, ((0, 0),) * len(lead) + ((0, nblocks * block_len - width),))
    blocks = padded.reshape(lead + (nblocks, block_len))
    block_total = jnp.sum(blocks, axis=-1)
    prefix = jnp.cumsum(blocks, axis=-1) - blocks
    count = nblocks - 8
    running = block_total[..., 0:count]
    for offset in range(1, 8):
        running = running + block_total[..., offset : offset + count]
    windows = running[..., None] - prefix[..., :count, :] + prefix[..., 8:, :]
    return windows.reshape(lead + (count * block_len,))[..., : width - span]


def window_norms(extended, span):
    values = extended.astype(jnp.float32)
    stacked = jnp.stack([values, values * values], axis=0)
    windows = box_sums(stacked, span)
    sums = windows[0]
    squares = windows[1]
    spread = (squares - sums * sums / span) / span
    inverse = 1.0 / (math.sqrt(span) * jnp.sqrt(jnp.maximum(spread, 0.0) + EPS))
    return inverse.astype(jnp.bfloat16)


def per_device(data, templates, stations, shifts, used):
    span = templates.shape[3]
    samples = data.shape[2]
    reach = span + MAXSHIFT
    whole = lax.all_gather(data, "tpl", axis=0, tiled=True)
    tail = passed_along(whole[:, :, :reach], "slab", -1)
    extended = jnp.concatenate([whole, tail], axis=2)
    inv_norm = window_norms(extended, span)
    norm_full = jnp.pad(inv_norm, ((0, 0), (0, 0), (0, extended.shape[2] - inv_norm.shape[2])))
    table = jnp.stack([extended, norm_full], axis=1)
    unit = normalize(templates)
    slots = templates.shape[1]
    initial = jnp.zeros((templates.shape[0] * lax.axis_size("slab"), samples), jnp.float32)
    tn = lax.all_gather(unit, "slab", axis=0, tiled=True)
    sta = lax.all_gather(stations, "slab", axis=0, tiled=True)
    sh = lax.all_gather(shifts, "slab", axis=0, tiled=True)
    count = lax.all_gather(used, "slab", axis=0, tiled=True)
    panel = tn.shape[0]
    flat_sta = sta.reshape(-1)
    flat_sh = sh.reshape(-1)
    rows = table[flat_sta]
    cut = jax.vmap(lambda r, s: lax.dynamic_slice_in_dim(r, s, samples + span - 1, 2))(
        rows, flat_sh
    )
    windows = cut[:, 0]
    norms = cut[:, 1, :, :samples]
    chans = panel * slots * tn.shape[2]
    corr = lax.conv_general_dilated(
        windows.reshape(1, chans, samples + span - 1),
        tn.reshape(chans, 1, span),
        (1,),
        "VALID",
        dimension_numbers=("NCH", "OIH", "NCH"),
        feature_group_count=chans,
        preferred_element_type=jnp.float32,
    )
    scaled = corr.reshape(panel, slots, tn.shape[2], samples) * norms.reshape(
        panel, slots, tn.shape[2], samples
    ).astype(jnp.float32)
    slot_ids = jnp.arange(slots, dtype=jnp.int32)[None, :]
    scale = jnp.sqrt(span / (3.0 * count.astype(jnp.float32)))[:, None]
    weight = jnp.where(slot_ids < count[:, None], scale, 0.0)
    stack = jnp.einsum("pkct,pk->pt", scaled, weight)
    return lax.dynamic_update_slice(initial, stack, (jnp.int32(0), jnp.int32(0)))


def solution(mesh):
    return jax.shard_map(
        per_device,
        mesh=mesh,
        in_specs=(
            P("tpl", None, "slab"),
            P(("tpl", "slab"), None, None, None),
            P(("tpl", "slab"), None),
            P(("tpl", "slab"), None),
            P(("tpl", "slab")),
        ),
        out_specs=P("tpl", "slab"),
        check_vma=False,
    )
```

profile of v0, /device:TPU:7, one launch (start us, length us, event | category | flops | bytes accessed | tf_op | source)
XLA Modules:
  0.0 1251.1 jit_solution(6764360261945465847)
XLA Ops:
  0.0 10.9 all_gather.15
  11.7 3.4 collective-permute-start
  15.2 20.5 %all-gather = s32[16,2,8]{2,1,0:T(2,128)S(1)} all-gather(s32[1,2,8]{2,1,0:T(2,128)} %bitcast.44), channel_id=1, replica_groups=mesh['slab'=16,'tpl'=2] {'slab'}, dimensions={0}, use_global_device_ids=true | all-gather | bytes 1088 | tf_op jit(solution)/shard_map/all_gather | solution.py:70
  35.8 19.1 %all-gather.1 = s32[16,2,8]{2,1,0:T(2,128)S(1)} all-gather(s32[1,2,8]{2,1,0:T(2,128)} %bitcast.45), channel_id=1, replica_groups=mesh['slab'=16,'tpl'=2] {'slab'}, dimensions={0}, use_global_device_ids=true | all-gather | bytes 1088 | tf_op jit(solution)/shard_map/all_gather | solution.py:71
  57.7 20.6 %all_gather.18 = bf16[32,8,3,512]{3,1,2,0:T(8,128)(2,1)S(1)} all-gather(bf16[2,8,3,512]{3,1,2,0:T(8,128)(2,1)S(1)} %fusion.17), channel_id=1, replica_groups=mesh['slab'=16,'tpl'=2] {'slab'}, dimensions={0}, use_global_device_ids=true | all-gather | bytes 835584 | tf_op jit(solution)/shard_map/all_gather | solution.py:69
  79.6 3.0 copy.43
  84.0 5.7 all-reduce.3
  90.9 2.8 pad_maximum_fusion
  93.7 6.5 copy.50
  100.2 5.9 pad.9.clone
  106.1 15.9 %copy_subtract_fusion = f32[2,128,3,36,64]{1,3,2,4,0:T(8,128)} fusion(f32[2,128,3,36,64]{1,4,3,2,0:T(8,128)} %bitcast.34), kind=kOutput, calls=%fused_computation.4 | output fusion | flops 113246208 | bytes 14155776 | tf_op jit(solution)/shard_map/jit(cumsum)/reduce_window_sum | solution.py:36
  122.0 4.1 reduce_sum.36
  126.2 6.3 slice_add_fusion
  132.5 16.8 %copy.36 = f32[2,128,3,28,64]{1,4,3,2,0:T(8,128)S(1)} copy(f32[2,128,3,28,64]{1,3,2,4,0:T(8,128)S(1)} %slice_add_fusion) | data formatting | bytes 11010048 | tf_op jit(solution)/shard_map/add | solution.py:41
  150.4 5.3 copy.39
  155.7 2.1 copy.38
  157.9 6.2 pad_maximum_fusion.1
  164.1 17.0 %gather_fusion = bf16[256,2,3,1792]{3,1,2,0:T(2,128)(2,1)} fusion(bf16[128,2,3,1792]{3,1,2,0:T(2,128)(2,1)S(1)} %pad_maximum_fusion.1, s32[1024]{0:T(1024)S(1)} %pad_clamp_fusion), kind=kCustom, calls=%fused_computation | custom fusion | bytes 11011072 | tf_op jit(solution)/shard_map/gather | solution.py:76
  181.1 850.3 %while.1 = (s32[]{:T(128)}, bf16[256,2,3,1792]{3,1,2,0:T(2,128)(2,1)}, s32[256,4]{0,1:T(4,128)S(1)}, bf16[256,2,3,1535]{3,2,1,0:T(4,128)(2,1)}, s32[]{:T(128)}) while((s32[]{:T(128)}, bf16[256,2,3,1792]{3,1,2,0:T(2,128)(2,1)}, s32[256,4]{0,1:T(4,128)S(1)}, bf16[256,2,3,1535]{3,2,1,0:T(4,128)(2,1)}, s32[]{:T(128)}) %tuple.22), condition=%wide.while_cond, body=%wide.while_body.sunk | while | flops 2 | bytes 80469 | solution.py:77
  198.4 2.0 constant_dynamic-slice_fusion.5
  201.7 2.0 constant_dynamic-slice_fusion.5
  221.7 2.0 constant_dynamic-slice_fusion.5
  228.3 2.0 constant_dynamic-slice_fusion.5
  231.7 2.0 constant_dynamic-slice_fusion.5
  235.0 2.0 constant_dynamic-slice_fusion.5
  248.3 2.0 constant_dynamic-slice_fusion.5
  251.6 2.0 constant_dynamic-slice_fusion.5
  264.9 2.0 constant_dynamic-slice_fusion.5
  268.2 2.0 constant_dynamic-slice_fusion.5
  284.8 2.0 constant_dynamic-slice_fusion.5
  294.8 2.0 constant_dynamic-slice_fusion.5
  314.7 2.0 constant_dynamic-slice_fusion.5
  328.0 2.0 constant_dynamic-slice_fusion.5
  338.0 2.0 constant_dynamic-slice_fusion.5
  347.9 2.0 constant_dynamic-slice_fusion.5
  354.5 2.0 constant_dynamic-slice_fusion.5
  377.8 2.0 constant_dynamic-slice_fusion.5
  384.4 2.0 constant_dynamic-slice_fusion.5
  404.3 2.0 constant_dynamic-slice_fusion.5
  421.0 2.0 constant_dynamic-slice_fusion.5
  427.6 2.0 constant_dynamic-slice_fusion.5
  440.9 2.0 constant_dynamic-slice_fusion.5
  447.5 2.0 constant_dynamic-slice_fusion.5
  450.8 2.0 constant_dynamic-slice_fusion.5
  457.5 2.0 constant_dynamic-slice_fusion.5
  460.8 2.0 constant_dynamic-slice_fusion.5
  464.1 2.0 constant_dynamic-slice_fusion.5
  467.4 2.0 constant_dynamic-slice_fusion.5
  477.4 2.0 constant_dynamic-slice_fusion.5
  484.0 2.0 constant_dynamic-slice_fusion.5
  494.0 2.0 constant_dynamic-slice_fusion.5
  513.9 2.0 constant_dynamic-slice_fusion.5
  527.2 2.0 constant_dynamic-slice_fusion.5
  533.9 2.0 constant_dynamic-slice_fusion.5
  567.1 2.0 constant_dynamic-slice_fusion.5
  570.4 2.0 constant_dynamic-slice_fusion.5
  1031.5 3.0 slice.61
  1034.4 3.7 slice.62
  1038.1 4.1 reshape_squeeze.4
  1042.3 12.2 copy.42
  1054.5 179.4 %fusion.20 = f32[1,768,1024]{1,0,2:T(1,128)} fusion(bf16[1,768,1535]{1,0,2:T(2,128)(2,1)} %copy.42, bf16[768,1,512]{0,1,2:T(2,128)(2,1)S(1)} %copy-done.1), kind=kOutput, calls=%fused_computation.52 | convolution fusion | flops 805306368 | bytes 6289920 | tf_op jit(solution)/shard_map/conv_general_dilated | solution.py:83
  1233.8 6.8 copy.44
  1240.6 3.1 reshape.148
  1243.7 6.2 fusion.2
  (1027 shorter events, 782.0 us)
Async XLA Ops:
  11.7 78.7 %collective-permute-start = (bf16[128,3,768]{2,0,1:T(8,128)(2,1)}, bf16[128,3,768]{2,0,1:T(8,128)(2,1)S(1)}, u32[]{:S(2)}, u32[]{:S(2)}) collective-permute-start(bf16[128,3,768]{2,0,1:T(8,128)(2,1)} %slice.83), channel_id=1, source_target_pairs={{2,0},{4,2},{6,4},{8,6},{10,8},{12,10},{14,12},{16,14},{18,16},{20... | collective-permute-start | bytes 1769480 | tf_op jit(solution)/shard_map/ppermute | solution.py:17
  78.3 4.3 copy-start.4
  78.3 5.5 copy-start.3
  155.7 2.1 copy-start
  1042.3 12.2 copy-start.1
  1243.7 6.2 copy-start.2
where the time goes:
time: 1270 us; the launch traced here: 1250 us
  local copies, waits for them, and re-layouts  941 us (74%)
  matrix products  180 us (14%)
  blocking collectives  76.7 us (6%)
  other arithmetic  46.6 us (4%)
    gather x1024, local copies, waits for them, and re-layouts  848 us
    conv_general_dilated x1, matrix products, per_device(): lax.conv_general_dilated(windows.reshape(1, chans, samples + span - 1), t...  179 us
  transfers between devices with their start and end apart: 1, of which 0 were waited for; matrix products, arithmetic and copies ran while one was open for 1% of the time, Pallas kernels for 0%

commit v1 on v0

v1 whole, which is shorter than its diff:
```python
import functools
import math

import jax
import jax.numpy as jnp
from jax import lax
from jax.experimental import pallas as pl
from jax.experimental.pallas import tpu as pltpu
from jax.sharding import PartitionSpec as P

MAXSHIFT = 256


EPS = 1e-05


def passed_along(value, axis, steps):
    count = lax.axis_size(axis)
    initial, last = (max(0, -steps), min(count, count - steps))
    return lax.ppermute(value, axis, [(source, source + steps) for source in range(initial, last)])


def normalize(templates):
    span = templates.shape[-1]
    rows = templates.astype(jnp.float32)
    centered = rows - jnp.mean(rows, axis=-1, keepdims=True)
    rms = jnp.sqrt(jnp.mean(centered * centered, axis=-1, keepdims=True) + EPS)
    return (centered / (rms * math.sqrt(span))).astype(jnp.bfloat16)


LANES = 128
STEP = 32
TURNS = LANES // STEP
GROUP = 8
PLANE = 16


def prepare(span, ext_ref, xs_ref, ns_ref, sums_rows):
    rows, width = ext_ref.shape
    block = 256
    reach = block + span
    taps = lax.broadcasted_iota(jnp.int32, (reach, block), 0)
    starts = lax.broadcasted_iota(jnp.int32, (reach, block), 1)
    band = jnp.where((taps >= starts) & (taps < starts + span), 1.0, 0.0).astype(jnp.bfloat16)
    nblocks = (width - span) // block
    root = math.sqrt(span)

    @pl.loop(0, rows // sums_rows)
    def _(step):
        at = pl.ds(pl.multiple_of(step * sums_rows, sums_rows), sums_rows)
        for row in range(width // LANES):
            xs_ref[at, row, :] = ext_ref[at, row * LANES : (row + 1) * LANES].astype(jnp.float32)
        for row in range(width // LANES, PLANE):
            xs_ref[at, row, :] = jnp.zeros((sums_rows, LANES), jnp.float32)
        for n in range(nblocks):
            values = ext_ref[at, n * block : n * block + reach]
            wide = values.astype(jnp.float32)
            square = wide * wide
            high = square.astype(jnp.bfloat16)
            low = (square - high.astype(jnp.float32)).astype(jnp.bfloat16)
            sums = jnp.dot(values, band, preferred_element_type=jnp.float32)
            squares = jnp.dot(high, band, preferred_element_type=jnp.float32)
            squares += jnp.dot(low, band, preferred_element_type=jnp.float32)
            spread = (squares - sums * sums / span) / span
            inverse = 1.0 / (root * jnp.sqrt(jnp.maximum(spread, 0.0) + EPS))
            inverse = inverse.astype(jnp.bfloat16).astype(jnp.float32)
            for half in range(block // LANES):
                ns_ref[at, n * (block // LANES) + half, :] = inverse[:, half * LANES : (half + 1) * LANES]


def kernel(span, chans, row_ref, shift_ref, live_ref, scale_ref, ext_ref, unit_ref, out_ref, xs_ref, ns_ref, left_ref, right_ref):
    prepare(span, ext_ref, xs_ref, ns_ref, 128)
    panel = out_ref.shape[0]
    parts = span // LANES
    lane = lax.broadcasted_iota(jnp.int32, (8, LANES), 1)
    lane_wide = lax.broadcasted_iota(jnp.int32, (STEP, LANES), 1)
    lag = lax.broadcasted_iota(jnp.int32, (STEP, LANES), 0)
    inside = lane_wide >= lag
    lane_part = lane // STEP
    zero_step = jnp.zeros((STEP, LANES), jnp.float32)

    def template(j, _):
        live = live_ref[j]

        def group(g, total):
            base = j * chans + g * GROUP
            for i in range(GROUP):
                index = base + i
                row = row_ref[index]
                shift = shift_ref[index]
                turned = []
                for part in range(parts):
                    line = jnp.broadcast_to(unit_ref[pl.ds(index * parts + part, 1), :], (STEP, LANES))
                    turned.append(pltpu.roll(line, 0, 1, stride=1, stride_axis=0))
                edges = [zero_step] + turned + [zero_step]
                for part in range(parts + 1):
                    piece = jnp.where(inside, edges[part + 1], edges[part])
                    right_ref[i * STEP : (i + 1) * STEP, part * LANES : (part + 1) * LANES] = piece.astype(jnp.bfloat16)
                lines = []
                for turn in range(TURNS):
                    offset = shift + STEP * turn
                    first = offset // LANES
                    rest = offset % LANES
                    keep = lane >= rest
                    loads = [xs_ref[row, pl.ds(first + part, 8), :] for part in range(parts + 2)]
                    lines.append([
                        pltpu.roll(jnp.where(keep, loads[part], loads[part + 1]), LANES - rest, 1)
                        for part in range(parts + 1)
                    ])
                for part in range(parts + 1):
                    for pair in range(TURNS // 2):
                        both = jnp.concatenate([lines[2 * pair][part], lines[2 * pair + 1][part]], axis=0)
                        at = i * STEP + pair * 16
                        left_ref[at : at + 16, part * LANES : (part + 1) * LANES] = both.astype(jnp.bfloat16)
            for four in range(GROUP // TURNS):
                at = slice(four * LANES, (four + 1) * LANES)
                corr = lax.dot_general(
                    left_ref[at, :], right_ref[at, :], (((1,), (1,)), ((), ())),
                    preferred_element_type=jnp.float32,
                )
                for i in range(TURNS):
                    kc = g * GROUP + four * TURNS + i
                    index = j * chans + kc
                    row = row_ref[index]
                    shift = shift_ref[index]
                    wanted = (lane_part == i) & (kc < live)
                    added = []
                    for turn in range(TURNS):
                        offset = shift + STEP * turn
                        first = offset // LANES
                        rest = offset % LANES
                        near = ns_ref[row, pl.ds(first, 8), :]
                        far = ns_ref[row, pl.ds(first + 1, 8), :]
                        norm = pltpu.roll(jnp.where(lane >= rest, near, far), LANES + STEP * i - rest, 1)
                        value = corr[i * STEP + 8 * turn : i * STEP + 8 * turn + 8, :]
                        added.append(jnp.where(wanted, value * norm, 0.0))
                    total = tuple(t + a for t, a in zip(total, added))
            return total

        zero = jnp.zeros((8, LANES), jnp.float32)
        total = lax.fori_loop(0, (live + GROUP - 1) // GROUP, group, (zero,) * TURNS)
        result = zero
        for turn in range(TURNS):
            value = total[turn]
            value = value + pltpu.roll(value, LANES // 2, 1)
            value = value + pltpu.roll(value, LANES // 4, 1)
            result = jnp.where(lane_part == turn, value, result)
        out_ref[j] = result * scale_ref[j]
        return 0

    lax.fori_loop(0, panel, template, 0)


def detect(ext, unit, rows, shifts, live, scale, span, samples):
    chans = unit.shape[0] // live.shape[0]
    smem = pl.BlockSpec(memory_space=pltpu.SMEM)
    vmem = pl.BlockSpec(memory_space=pltpu.VMEM)
    panel = live.shape[0]
    return pl.pallas_call(
        functools.partial(kernel, span, chans),
        out_shape=jax.ShapeDtypeStruct((panel, samples // LANES, LANES), jnp.float32),
        in_specs=[smem, smem, smem, smem, vmem, vmem],
        out_specs=vmem,
        scratch_shapes=[
            pltpu.VMEM((ext.shape[0], PLANE, LANES), jnp.float32),
            pltpu.VMEM((ext.shape[0], PLANE, LANES), jnp.float32),
            pltpu.VMEM((GROUP * STEP, span + LANES), jnp.bfloat16),
            pltpu.VMEM((GROUP * STEP, span + LANES), jnp.bfloat16),
        ],
        compiler_params=pltpu.CompilerParams(vmem_limit_bytes=56 << 20),
    )(rows, shifts, live, scale, ext, unit.reshape(-1, LANES).astype(jnp.float32))


def per_device(data, templates, stations, shifts, used):
    span = templates.shape[3]
    comps = data.shape[1]
    samples = data.shape[2]
    reach = span + MAXSHIFT
    local = data.reshape(-1, samples)
    whole = lax.all_gather(local, "tpl", axis=0, tiled=True)
    tail = passed_along(whole[:, :reach], "slab", -1)
    extended = jnp.concatenate([whole, tail], axis=1)
    slots = templates.shape[1]
    unit = normalize(templates).reshape(-1, span)
    tn = lax.all_gather(unit, "slab", axis=0, tiled=True)
    lists = jnp.concatenate([stations, shifts, used[:, None]], axis=1)
    lists = lax.all_gather(lists, "slab", axis=0, tiled=True)
    sta = lists[:, :slots]
    sh = lists[:, slots : 2 * slots]
    count = lists[:, 2 * slots]
    rows = (sta[:, :, None] * comps + jnp.arange(comps, dtype=jnp.int32)).reshape(-1)
    moves = jnp.repeat(sh.reshape(-1), comps)
    scale = jnp.sqrt(span / (3.0 * count.astype(jnp.float32)))
    stack = detect(extended, tn, rows, moves, count * comps, scale, span, samples)
    return stack.reshape(-1, samples)


def solution(mesh):
    return jax.shard_map(
        per_device,
        mesh=mesh,
        in_specs=(
            P("tpl", None, "slab"),
            P(("tpl", "slab"), None, None, None),
            P(("tpl", "slab"), None),
            P(("tpl", "slab"), None),
            P(("tpl", "slab")),
        ),
        out_specs=P("tpl", "slab"),
        check_vma=False,
    )
```

time: 1270 us -> 124 us (0.10); the launches traced: 1250 us -> 125 us
  local copies, waits for them, and re-layouts: 941 us -> 7 us
  matrix products: 180 us -> 0 us
  Pallas kernels: 0 us -> 59.6 us
  other arithmetic: 46.6 us -> 2.99 us
  blocking collectives: 76.7 us -> 51.9 us
    gather x1025 -> x0, local copies, waits for them, and re-layouts: 865 us -> none
    conv_general_dilated x1 -> x0, matrix products: 179 us -> none  [per_device(): lax.conv_general_dilated(windows.reshape(1, chans, samples + span - 1), t...]
    pallas_call x0 -> x1, Pallas kernels: none -> 59.6 us  [detect(): pl.pallas_call(functools.partial(kernel, span, chans), out_shape=jax.Shap...]
    another operation x4 -> x0, other arithmetic: 25 us -> none  [the longest x1 15.9 us: box_sums(): prefix = jnp.cumsum(blocks, axis=-1) - blocks]
    another operation x5 -> x0, local copies, waits for them, and re-layouts: 23.8 us -> none  [the longest x2 16.3 us: per_device(): windows.reshape(1, chans, samples + span - 1)]
    all_gather x3 -> x2, blocking collectives: 50.4 us -> 30.7 us  [the longest x1 20.1 us: per_device(): lists = lax.all_gather(lists, 'slab', axis=0, tiled=True)]
    add x1, local copies, waits for them, and re-layouts: 16.8 us -> 0.8 us  [per_device(): sta[:, :, None] * comps + jnp.arange(comps, dtype=jnp.int32)]
  transfers between devices with their start and end apart: 1 -> 1, of which waited for: 0 -> 0; matrix products, arithmetic and copies ran while one was open for 1% -> 4% of each run, Pallas kernels for 0% -> 0%
where the time goes in v1:
time: 124 us; the launch traced here: 125 us
  Pallas kernels  59.6 us (48%)
  blocking collectives  51.9 us (42%)
  local copies, waits for them, and re-layouts  7 us (6%)
  starting transfers between devices  3.46 us (3%)
  other arithmetic  2.99 us (2%)
    pallas_call x1, Pallas kernels, detect(): pl.pallas_call(functools.partial(kernel, span, chans), out_shape=jax.Shap...  59.6 us
    all_gather x1, blocking collectives, per_device(): tn = lax.all_gather(unit, 'slab', axis=0, tiled=True)  21.2 us
    all_gather x1, blocking collectives, per_device(): lists = lax.all_gather(lists, 'slab', axis=0, tiled=True)  20.1 us
    all_gather x1, blocking collectives, per_device(): whole = lax.all_gather(local, 'tpl', axis=0, tiled=True)  10.7 us
    ppermute x1, starting transfers between devices, passed_along(): lax.ppermute(value, axis, [(source, source + steps) for source in range(i...  3.46 us
    unnamed x11, local copies, waits for them, and re-layouts  3.02 us
  transfers between devices with their start and end apart: 1, of which 0 were waited for; matrix products, arithmetic and copies ran while one was open for 4% of the time, Pallas kernels for 0%

profile of v1, /device:TPU:7, one launch (start us, length us, event | category | flops | bytes accessed | tf_op | source)
XLA Modules:
  0.0 125.0 jit_solution(16912274434465938563)
XLA Ops:
  0.0 1.3 %copy.15 = bf16[64,3,1024]{2,1,0:T(4,128)(2,1)S(1)} copy(bf16[64,3,1024]{2,0,1:T(8,128)(2,1)} %param.5) | data formatting | bytes 786432 | tf_op args[0]
  1.3 0.0 copy-start.3
  1.3 0.0 copy-start.1
  1.4 0.0 copy-start.2
  1.4 0.0 copy-start
  1.4 0.3 reshape.48
  1.7 10.7 %all_gather.10 = bf16[384,1024]{1,0:T(8,128)(2,1)S(1)} all-gather(bf16[192,1024]{1,0:T(8,128)(2,1)S(1)} %reshape.48), channel_id=1, replica_groups=mesh['slab'=16,'tpl'=2] {'tpl'}, dimensions={0}, use_global_device_ids=true | all-gather | bytes 1179648 | tf_op jit(solution)/shard_map/all_gather | solution.py:180
  12.4 0.1 slice.19
  12.4 3.5 %collective-permute-start = (bf16[384,768]{1,0:T(8,128)(2,1)S(1)}, bf16[384,768]{1,0:T(8,128)(2,1)S(1)}, u32[]{:S(2)}, u32[]{:S(2)}) collective-permute-start(bf16[384,768]{1,0:T(8,128)(2,1)S(1)} %slice.19), channel_id=1, source_target_pairs={{2,0},{4,2},{6,4},{8,6},{10,8},{12,10},{14,12},{16,14},{18,16},{20... | collective-permute-start | bytes 1769480 | tf_op jit(solution)/shard_map/ppermute | solution.py:20
  15.9 0.0 copy-done.3
  15.9 0.1 copy.13
  16.0 0.0 copy-done.1
  16.0 0.0 copy-done.2
  16.0 0.1 add_bitcast_fusion
  16.1 20.1 %all-gather = s32[16,2,17]{2,1,0:T(2,128)S(1)} all-gather(s32[1,2,17]{2,1,0:T(2,128)S(1)} %add_bitcast_fusion), channel_id=1, replica_groups=mesh['slab'=16,'tpl'=2] {'slab'}, dimensions={0}, use_global_device_ids=true | all-gather | bytes 2312 | tf_op jit(solution)/shard_map/all_gather | solution.py:187
  36.2 0.1 fusion.4
  36.2 0.1 slice.18
  36.3 0.0 copy-done
  36.3 0.1 convert_reduce_fusion
  36.4 0.2 fusion.2
  36.6 0.1 fusion.3
  36.8 21.2 %all_gather.11 = bf16[768,512]{1,0:T(8,128)(2,1)S(1)} all-gather(bf16[48,512]{1,0:T(8,128)(2,1)S(1)} %reshape.49), channel_id=1, replica_groups=mesh['slab'=16,'tpl'=2] {'slab'}, dimensions={0}, use_global_device_ids=true | all-gather | bytes 835584 | tf_op jit(solution)/shard_map/all_gather | solution.py:185
  58.0 1.6 %reshape.51.unit_ref = f32[3072,128]{1,0:T(8,128)} reshape(bf16[768,512]{1,0:T(8,128)(2,1)S(1)} %all_gather.11) | data formatting | bytes 2359296 | tf_op jit(solution)/shard_map/convert_element_type | solution.py:171
  59.5 0.1 reshape.46
  59.6 0.1 broadcast_in_dim.5
  59.7 0.8 reshape.47.shift_ref
  60.5 0.1 iota_add_fusion
  60.6 0.8 add.31.row_ref
  61.4 0.1 copy.17
  61.5 0.6 multiply_bitcast_fusion.live_ref
  62.1 0.6 sqrt_bitcast_fusion.scale_ref
  62.7 0.0 collective-permute-done
  62.7 1.2 pad_maximum_fusion.ext_ref
  63.9 59.6 %shard_map.55 = f32[32,8,128]{2,1,0:T(8,128)} custom-call(s32[768]{0:T(1024)} %add.31.row_ref, s32[768]{0:T(1024)} %reshape.47.shift_ref, s32[32]{0:T(128)} %multiply_bitcast_fusion.live_ref, f32[32]{0:T(128)} %sqrt_bitcast_fusion.scale_ref, bf16[384,1792]{1,0:T(8,128)(2,1)} %pad_maximum_fusion.ext_ref, f32[3072,128]{1,0:T(8,128)} %reshape.51.unit_ref), custom_call_target="tpu_custom_call" | custom-call | tf_op jit(solution)/shard_map/pallas_call | solution.py:159
  123.4 1.6 %copy.20 = f32[4,8,8,128]{3,1,2,0:T(8,128)} copy(f32[4,8,8,128]{3,2,1,0:T(8,128)} %bitcast.12) | data formatting | bytes 262144
  (4 shorter events, 0.1 us)
Async XLA Ops:
  1.3 14.6 %copy-start.3 = (s32[2]{0:T(128)S(1)}, s32[2]{0:T(128)}, u32[]{:S(2)}) copy-start(s32[2]{0:T(128)} %param.9) | copy-start | bytes 28
  1.3 14.7 %copy-start.1 = (s32[2,8]{1,0:T(2,128)S(1)}, s32[2,8]{1,0:T(2,128)}, u32[]{:S(2)}) copy-start(s32[2,8]{1,0:T(2,128)} %param.8) | copy-start | bytes 196
  1.4 14.6 %copy-start.2 = (s32[2,8]{1,0:T(2,128)S(1)}, s32[2,8]{1,0:T(2,128)}, u32[]{:S(2)}) copy-start(s32[2,8]{1,0:T(2,128)} %param.7) | copy-start | bytes 196
  1.4 34.9 %copy-start = (bf16[2,8,3,512]{3,1,2,0:T(8,128)(2,1)S(1)}, bf16[2,8,3,512]{3,1,2,0:T(8,128)(2,1)}, u32[]{:S(2)}) copy-start(bf16[2,8,3,512]{3,1,2,0:T(8,128)(2,1)} %param.6) | copy-start | bytes 147460
  12.4 50.3 %collective-permute-start = (bf16[384,768]{1,0:T(8,128)(2,1)S(1)}, bf16[384,768]{1,0:T(8,128)(2,1)S(1)}, u32[]{:S(2)}, u32[]{:S(2)}) collective-permute-start(bf16[384,768]{1,0:T(8,128)(2,1)S(1)} %slice.19), channel_id=1, source_target_pairs={{2,0},{4,2},{6,4},{8,6},{10,8},{12,10},{14,12},{16,14},{18,16},{20... | collective-permute-start | bytes 1769480 | tf_op jit(solution)/shard_map/ppermute | solution.py:20
